TPU v7x, 512 devices: a whole 4x4x16 slice. The times are simulated.
512 devices in a mesh: seq: 64 (over z, y), dp: 8 (over x, core).
Axes of the slice: x: 4, y: 4, z: 16, core: 2. Of those that a mesh axis runs over, the one named last changes fastest.
Arguments:
- queries: bfloat16 [8, 8192, 2048], P('dp', 'seq'), may hold values from -40 to 40
- keys: bfloat16 [8, 8192, 2048], P('dp', 'seq'), may hold values from -6 to 6
- values: bfloat16 [8, 8192, 2048], P('dp', 'seq'), may hold values from -6 to 6
- grad_out: bfloat16 [8, 8192, 2048], P('dp', 'seq'), may hold values from -48 to 48
- lengths: int32 [8], P('dp'), may hold values from 1024 to 8192, as said below
- fields: int32 [8, 8192], P('dp', 'seq'), may hold values from 0 to 63
- field_bias: bfloat16 [16, 64], replicated, may hold values from -6 to 6
Outputs:
- grad_queries: bfloat16 [8, 8192, 2048], P('dp', 'seq')
- grad_keys: bfloat16 [8, 8192, 2048], P('dp', 'seq')
- grad_values: bfloat16 [8, 8192, 2048], P('dp', 'seq')
- grad_bias: float32 [16, 64], replicated
Inputs may be any that keep to these rules, and one draw needn't show every extreme that they name: `lengths`: the valid positions of a sequence form a prefix; in every draw some sequence is full.
All inputs are finite; a program needn't handle non-finite values.
Results may differ from a plain program's by a relative error of at most 0.0077.
Values may be sent and summed in bfloat16 or wider, within the bound.
A program may use at most 128 MiB of HBM per device.

v0:
```python
import jax
import jax.numpy as jnp
from jax import lax
from jax.sharding import PartitionSpec as P

HEADS = 16
HEAD_DIM = 128
WINDOW = 512
FIELDS = 64


def passed_along(value, axis, steps):
    count = lax.axis_size(axis)
    first, last = (max(0, -steps), min(count, count - steps))
    return lax.ppermute(value, axis, [(source, source + steps) for source in range(first, last)])


def split_heads(rows):
    return rows.reshape(rows.shape[0], HEADS, HEAD_DIM)


def band_mask(query_places, key_places, length):
    not_after = key_places[None, :] <= query_places[:, None]
    inside = key_places[None, :] > query_places[:, None] - WINDOW
    started = key_places[None, :] >= 0
    live_rows = query_places[:, None] < length
    return not_after & inside & started & live_rows


def logits_of(query_heads, key_heads, key_bias):
    factor = HEAD_DIM ** (-0.5)
    products = jnp.einsum(
        "qhd,khd->hqk", query_heads, key_heads, preferred_element_type=jnp.float32
    )
    return products * factor + key_bias[:, None, :]


def grad_logits_of(attn_weights, row_delta, grad_heads, value_heads):
    grad_probs = jnp.einsum(
        "qhd,khd->hqk", grad_heads, value_heads, preferred_element_type=jnp.float32
    )
    return attn_weights * (grad_probs - row_delta[:, :, None])


def shards(queries, keys, values, grad_out, lengths, fields, field_bias):
    tok_rows = queries.shape[1]
    row_width = queries.shape[2]
    length = lengths[0]
    query_own = queries[0]
    key_own = keys[0]
    value_own = values[0]
    grad_own = grad_out[0]
    reach_blocks = WINDOW // tok_rows
    factor = HEAD_DIM ** (-0.5)
    block_index = lax.axis_index("seq")
    onehot = (fields[0][:, None] == jnp.arange(FIELDS, dtype=jnp.int32)[None, :]).astype(
        jnp.bfloat16
    )
    own_bias = jnp.dot(field_bias, onehot.T, preferred_element_type=jnp.float32).astype(
        jnp.bfloat16
    )
    package = (key_own, value_own, own_bias)
    arrived = []
    for distance in range(1, reach_blocks + 1):
        arrived.append(passed_along((package[0], package[1], package[2]), "seq", distance))
    ordered = arrived[::-1] + [package]
    key_all = jnp.concatenate([arrival[0] for arrival in ordered], axis=0)
    value_all = jnp.concatenate([arrival[1] for arrival in ordered], axis=0)
    bias_all = jnp.concatenate([arrival[2] for arrival in ordered], axis=1).astype(jnp.float32)
    query_places = block_index * tok_rows + jnp.arange(tok_rows, dtype=jnp.int32)
    key_places = (block_index - reach_blocks) * tok_rows + jnp.arange(
        (reach_blocks + 1) * tok_rows, dtype=jnp.int32
    )
    query_heads = split_heads(query_own)
    grad_heads = split_heads(grad_own)
    key_heads = split_heads(key_all)
    value_heads = split_heads(value_all)
    logits = logits_of(query_heads, key_heads, bias_all)
    visible = band_mask(query_places, key_places, length)[None]
    live_rows = (query_places < length)[None, :, None]
    row_peak = jnp.max(jnp.where(visible, logits, -1e30), axis=2, keepdims=True)
    powers = jnp.where(visible, jnp.exp(logits - row_peak), 0.0)
    totals = jnp.where(live_rows, jnp.sum(powers, axis=2, keepdims=True), 1.0)
    attn_weights = powers / totals
    weights_low = attn_weights.astype(jnp.bfloat16)
    outputs = jnp.einsum(
        "hqk,khd->qhd", weights_low, value_heads, preferred_element_type=jnp.float32
    )
    row_delta = jnp.einsum("qhd,qhd->hq", grad_heads.astype(jnp.float32), outputs)
    grad_logits = grad_logits_of(attn_weights, row_delta, grad_heads, value_heads)
    grad_low = grad_logits.astype(jnp.bfloat16)
    grad_query = (
        jnp.einsum("hqk,khd->qhd", grad_low, key_heads, preferred_element_type=jnp.float32) * factor
    )
    own_cols = reach_blocks * tok_rows
    grad_key = (
        jnp.einsum(
            "hqk,qhd->khd", grad_low, query_heads, preferred_element_type=jnp.float32
        ).reshape(-1, row_width)
        * factor
    )
    grad_value = jnp.einsum(
        "hqk,qhd->khd", weights_low, grad_heads, preferred_element_type=jnp.float32
    ).reshape(-1, row_width)
    column = jnp.sum(grad_logits, axis=1)
    key_total = grad_key[own_cols:]
    value_total = grad_value[own_cols:]
    column_total = column[:, own_cols:]
    for distance in range(1, reach_blocks + 1):
        first_row = (reach_blocks - distance) * tok_rows
        returned = passed_along(
            (
                grad_key[first_row : first_row + tok_rows],
                grad_value[first_row : first_row + tok_rows],
                column[:, first_row : first_row + tok_rows],
            ),
            "seq",
            -distance,
        )
        key_total = key_total + returned[0]
        value_total = value_total + returned[1]
        column_total = column_total + returned[2]
    bias_local = jnp.dot(column_total, onehot.astype(jnp.float32), precision=lax.Precision.HIGHEST)
    query_low = grad_query.reshape(tok_rows, row_width).astype(jnp.bfloat16)
    key_low = key_total.astype(jnp.bfloat16)
    value_low = value_total.astype(jnp.bfloat16)
    bias_total = lax.psum(bias_local, ("seq", "dp"))
    return (
        query_low.reshape(1, tok_rows, row_width),
        key_low.reshape(1, tok_rows, row_width),
        value_low.reshape(1, tok_rows, row_width),
        bias_total,
    )


def solution(mesh):
    return jax.shard_map(
        shards,
        mesh=mesh,
        in_specs=(
            P("dp", "seq", None),
            P("dp", "seq", None),
            P("dp", "seq", None),
            P("dp", "seq", None),
            P("dp"),
            P("dp", "seq"),
            P(),
        ),
        out_specs=(P("dp", "seq", None), P("dp", "seq", None), P("dp", "seq", None), P()),
        check_vma=False,
    )
```

profile of v0, /device:TPU:1, one launch (start us, length us, event | category | flops | bytes accessed | tf_op | source)
XLA Modules:
  0.0 491.5 jit_solution(1476968906301964713)
XLA Ops:
  2.2 4.2 collective-permute-start.7
  6.4 4.5 collective-permute-start.6
  10.9 1.3 copy.35
  12.2 2.6 collective-permute-start.11
  14.9 4.8 collective-permute-start.10
  19.7 4.2 collective-permute-start.9
  24.6 2.6 collective-permute-start.5
  27.3 4.8 collective-permute-start.4
  32.3 1.3 copy.27
  38.1 5.2 %collective-permute-done.5 = bf16[16,128]{1,0:T(8,128)(2,1)S(1)} collective-permute-done((bf16[16,128]{1,0:T(8,128)(2,1)S(1)}, bf16[16,128]{1,0:T(8,128)(2,1)S(1)}, u32[]{:S(2)}, u32[]{:S(2)}) %collective-permute-start.5) | collective-permute-done | bytes 4128 | tf_op jit(solution)/shard_map/ppermute | solution.py:15
  44.7 18.3 %collective-permute-start.3 = (bf16[128,2048]{0,1:T(8,128)(2,1)S(1)}, bf16[128,2048]{0,1:T(8,128)(2,1)}, u32[]{:S(2)}, u32[]{:S(2)}) collective-permute-start(bf16[128,2048]{0,1:T(8,128)(2,1)S(1)} %bitcast.102), channel_id=1, source_target_pairs={{0,8},{8,16},{16,24},{24,32},{32,40},{40,48},{48,56},{56,64},{64,7... | collective-permute-start | bytes 1572872 | tf_op jit(solution)/shard_map/ppermute | solution.py:15
  63.0 9.7 %collective-permute-start.2 = (bf16[128,2048]{0,1:T(8,128)(2,1)S(1)}, bf16[128,2048]{0,1:T(8,128)(2,1)}, u32[]{:S(2)}, u32[]{:S(2)}) collective-permute-start(bf16[128,2048]{0,1:T(8,128)(2,1)S(1)} %bitcast.103), channel_id=1, source_target_pairs={{0,16},{8,24},{16,32},{24,40},{32,48},{40,56},{48,64},{56,72},{64,... | collective-permute-start | bytes 1572872 | tf_op jit(solution)/shard_map/ppermute | solution.py:15
  72.7 5.3 %collective-permute-start.1 = (bf16[128,2048]{0,1:T(8,128)(2,1)S(1)}, bf16[128,2048]{0,1:T(8,128)(2,1)}, u32[]{:S(2)}, u32[]{:S(2)}) collective-permute-start(bf16[128,2048]{0,1:T(8,128)(2,1)S(1)} %bitcast.104), channel_id=1, source_target_pairs={{0,24},{8,32},{16,40},{24,48},{32,56},{40,64},{48,72},{56,80},{64,... | collective-permute-start | bytes 1572872 | tf_op jit(solution)/shard_map/ppermute | solution.py:15
  78.0 2.1 collective-permute-start
  82.3 2.0 copy.38
  85.4 2.0 copy.32
  87.4 2.0 copy.31
  89.5 4.0 collective-permute-done.1
  93.5 2.0 copy.30
  95.5 1.3 copy.29
  98.8 2.0 constant_dynamic-update-slice_fusion.3
  100.8 2.0 constant_dynamic-update-slice_fusion.2
  104.6 7.6 %fusion.34 = (f32[16,128]{1,0:T(8,128)S(1)}, f32[16,128,640]{1,2,0:T(8,128)}) fusion(f32[16,640]{1,0:T(8,128)S(1)} %convert_element_type.46, pred[128,640]{0,1:T(8,128)(4,1)S(1)} %and_and_fusion, bf16[640,16,128]{2,0,1:T(8,128)(2,1)} %constant_dynamic-update-slice_fusion, bf16[128,16,128]{0,2,1:T(8,128)(2,1)} %bitcast.94), kind=kOutput, calls=%fused_computation.67 | convolution fusion | flops 681575040 | bytes 8519680 | tf_op jit(solution)/shard_map/sub | solution.py:82
  115.8 1.5 copy-done.5
  117.3 3.3 fusion.8
  120.6 2.0 convolution_bitcast_fusion.1
  122.6 2.6 copy.69
  125.2 1.6 multiply_reduce_fusion
  126.9 5.2 %fusion.35 = (f32[16,640]{1,0:T(8,128)S(1)}, bf16[16,128,640]{1,2,0:T(8,128)(2,1)S(1)}) fusion(f32[16,128]{1,0:T(8,128)S(1)} %copy.70, bf16[640,16,128]{2,0,1:T(8,128)(2,1)} %copy-done.5, bf16[128,16,128]{0,2,1:T(8,128)(2,1)} %copy.55, f32[16,128,640]{1,2,0:T(8,128)} %get-tuple-element.27, f32[16,128]{1,0:T(8,128)S(1)} %broadcast_select_fusion), kind=kOutput, calls=%fused_computation.68 | convolution fusion | flops 342087680 | bytes 11067392 | tf_op jit(solution)/shard_map/qhd,khd->hqk/dot_general | solution.py:39
  133.5 2.4 fusion.32
  135.9 2.5 copy.52
  138.4 2.5 copy.51
  141.0 2.6 copy.50
  150.1 2.6 copy.53
  152.6 15.2 %collective-permute-done.20 = f32[16,128]{1,0:T(8,128)S(1)} collective-permute-done((f32[16,128]{1,0:T(8,128)S(1)}, f32[16,128]{1,0:T(8,128)S(1)}, u32[]{:S(2)}, u32[]{:S(2)}) %collective-permute-start.20) | collective-permute-done | bytes 8224 | tf_op jit(solution)/shard_map/ppermute | solution.py:15
  169.2 109.7 %collective-permute-done.23 = f32[16,128]{1,0:T(8,128)S(1)} collective-permute-done((f32[16,128]{1,0:T(8,128)S(1)}, f32[16,128]{1,0:T(8,128)S(1)}, u32[]{:S(2)}, u32[]{:S(2)}) %collective-permute-start.23) | collective-permute-done | bytes 8224 | tf_op jit(solution)/shard_map/ppermute | solution.py:15
  281.2 2.8 collective-permute-done.22
  284.0 1.5 collective-permute-start.21
  285.5 2.0 fusion.31
  287.5 1.4 copy.56
  288.8 1.4 copy.60
  290.2 2.7 copy.59
  292.9 2.6 copy.58
  300.7 2.8 fusion.11
  304.5 1.6 copy.57
  306.6 178.1 %psum.7 = f32[16,64]{1,0:T(8,128)} all-reduce(f32[16,64]{1,0:T(8,128)S(1)} %fusion.22), channel_id=1, replica_groups=mesh['seq'=64,'dp'=8] {'seq','dp'}, use_global_device_ids=true, to_apply=%region_3.4 | all-reduce | flops 1024 | bytes 8192 | tf_op jit(solution)/shard_map/psum | solution.py:127
  484.7 2.4 fusion.18
  488.1 3.4 fusion.19
  (97 shorter events, 37.5 us)
Async XLA Ops:
  0.6 0.7 copy-start
  0.6 35.0 %copy-start.12 = (bf16[1,128,2048]{2,1,0:T(8,128)(2,1)S(1)}, bf16[1,128,2048]{2,1,0:T(8,128)(2,1)}, u32[]{:S(2)}) copy-start(bf16[1,128,2048]{2,1,0:T(8,128)(2,1)} %param.7) | copy-start | bytes 1572868
  2.2 34.5 %copy-start.13 = (bf16[1,128,2048]{2,1,0:T(8,128)(2,1)S(1)}, bf16[1,128,2048]{2,1,0:T(8,128)(2,1)}, u32[]{:S(2)}) copy-start(bf16[1,128,2048]{2,1,0:T(8,128)(2,1)} %param.10) | copy-start | bytes 1572868
  2.2 22.4 %collective-permute-start.7 = (bf16[16,128]{1,0:T(8,128)(2,1)S(1)}, bf16[16,128]{1,0:T(8,128)(2,1)S(1)}, u32[]{:S(2)}, u32[]{:S(2)}) collective-permute-start(bf16[16,128]{1,0:T(8,128)(2,1)S(1)} %fusion.14), channel_id=1, source_target_pairs={{0,8},{8,16},{16,24},{24,32},{32,40},{40,48},{48,56},{56,64},{64,7... | collective-permute-start | bytes 12296 | tf_op jit(solution)/shard_map/ppermute | solution.py:15
  6.4 20.9 %collective-permute-start.6 = (bf16[16,128]{1,0:T(8,128)(2,1)S(1)}, bf16[16,128]{1,0:T(8,128)(2,1)S(1)}, u32[]{:S(2)}, u32[]{:S(2)}) collective-permute-start(bf16[16,128]{1,0:T(8,128)(2,1)S(1)} %fusion.14), channel_id=1, source_target_pairs={{0,16},{8,24},{16,32},{24,40},{32,48},{40,56},{48,64},{56,72},{64,... | collective-permute-start | bytes 12296 | tf_op jit(solution)/shard_map/ppermute | solution.py:15
  12.2 50.8 %collective-permute-start.11 = (bf16[128,2048]{0,1:T(8,128)(2,1)S(1)}, bf16[128,2048]{0,1:T(8,128)(2,1)S(1)}, u32[]{:S(2)}, u32[]{:S(2)}) collective-permute-start(bf16[128,2048]{0,1:T(8,128)(2,1)S(1)} %bitcast.96), channel_id=1, source_target_pairs={{0,8},{8,16},{16,24},{24,32},{32,40},{40,48},{48,56},{56,64},{64,7... | collective-permute-start | bytes 1572872 | tf_op jit(solution)/shard_map/ppermute | solution.py:15
  14.9 57.8 %collective-permute-start.10 = (bf16[128,2048]{0,1:T(8,128)(2,1)S(1)}, bf16[128,2048]{0,1:T(8,128)(2,1)S(1)}, u32[]{:S(2)}, u32[]{:S(2)}) collective-permute-start(bf16[128,2048]{0,1:T(8,128)(2,1)S(1)} %bitcast.97), channel_id=1, source_target_pairs={{0,16},{8,24},{16,32},{24,40},{32,48},{40,56},{48,64},{56,72},{64,... | collective-permute-start | bytes 1572872 | tf_op jit(solution)/shard_map/ppermute | solution.py:15
  19.7 58.3 %collective-permute-start.9 = (bf16[128,2048]{0,1:T(8,128)(2,1)S(1)}, bf16[128,2048]{0,1:T(8,128)(2,1)}, u32[]{:S(2)}, u32[]{:S(2)}) collective-permute-start(bf16[128,2048]{0,1:T(8,128)(2,1)S(1)} %bitcast.98), channel_id=1, source_target_pairs={{0,24},{8,32},{16,40},{24,48},{32,56},{40,64},{48,72},{56,80},{64,... | collective-permute-start | bytes 1572872 | tf_op jit(solution)/shard_map/ppermute | solution.py:15
  24.6 18.7 %collective-permute-start.5 = (bf16[16,128]{1,0:T(8,128)(2,1)S(1)}, bf16[16,128]{1,0:T(8,128)(2,1)S(1)}, u32[]{:S(2)}, u32[]{:S(2)}) collective-permute-start(bf16[16,128]{1,0:T(8,128)(2,1)S(1)} %fusion.14), channel_id=1, source_target_pairs={{0,24},{8,32},{16,40},{24,48},{32,56},{40,64},{48,72},{56,80},{64,... | collective-permute-start | bytes 12296 | tf_op jit(solution)/shard_map/ppermute | solution.py:15
  27.3 17.4 %collective-permute-start.4 = (bf16[16,128]{1,0:T(8,128)(2,1)S(1)}, bf16[16,128]{1,0:T(8,128)(2,1)S(1)}, u32[]{:S(2)}, u32[]{:S(2)}) collective-permute-start(bf16[16,128]{1,0:T(8,128)(2,1)S(1)} %fusion.14), channel_id=1, source_target_pairs={{0,32},{8,40},{16,48},{24,56},{32,64},{40,72},{48,80},{56,88},{64,... | collective-permute-start | bytes 12296 | tf_op jit(solution)/shard_map/ppermute | solution.py:15
  43.3 41.0 %collective-permute-start.8 = (bf16[128,2048]{0,1:T(8,128)(2,1)S(1)}, bf16[128,2048]{0,1:T(8,128)(2,1)S(1)}, u32[]{:S(2)}, u32[]{:S(2)}) collective-permute-start(bf16[128,2048]{0,1:T(8,128)(2,1)S(1)} %bitcast.100), channel_id=1, source_target_pairs={{0,32},{8,40},{16,48},{24,56},{32,64},{40,72},{48,80},{56,88},{64,... | collective-permute-start | bytes 1572872 | tf_op jit(solution)/shard_map/ppermute | solution.py:15
  44.7 40.7 %collective-permute-start.3 = (bf16[128,2048]{0,1:T(8,128)(2,1)S(1)}, bf16[128,2048]{0,1:T(8,128)(2,1)}, u32[]{:S(2)}, u32[]{:S(2)}) collective-permute-start(bf16[128,2048]{0,1:T(8,128)(2,1)S(1)} %bitcast.102), channel_id=1, source_target_pairs={{0,8},{8,16},{16,24},{24,32},{32,40},{40,48},{48,56},{56,64},{64,7... | collective-permute-start | bytes 1572872 | tf_op jit(solution)/shard_map/ppermute | solution.py:15
  63.0 24.4 %collective-permute-start.2 = (bf16[128,2048]{0,1:T(8,128)(2,1)S(1)}, bf16[128,2048]{0,1:T(8,128)(2,1)}, u32[]{:S(2)}, u32[]{:S(2)}) collective-permute-start(bf16[128,2048]{0,1:T(8,128)(2,1)S(1)} %bitcast.103), channel_id=1, source_target_pairs={{0,16},{8,24},{16,32},{24,40},{32,48},{40,56},{48,64},{56,72},{64,... | collective-permute-start | bytes 1572872 | tf_op jit(solution)/shard_map/ppermute | solution.py:15
  72.7 20.8 %collective-permute-start.1 = (bf16[128,2048]{0,1:T(8,128)(2,1)S(1)}, bf16[128,2048]{0,1:T(8,128)(2,1)}, u32[]{:S(2)}, u32[]{:S(2)}) collective-permute-start(bf16[128,2048]{0,1:T(8,128)(2,1)S(1)} %bitcast.104), channel_id=1, source_target_pairs={{0,24},{8,32},{16,40},{24,48},{32,56},{40,64},{48,72},{56,80},{64,... | collective-permute-start | bytes 1572872 | tf_op jit(solution)/shard_map/ppermute | solution.py:15
  78.0 17.5 %collective-permute-start = (bf16[128,2048]{0,1:T(8,128)(2,1)S(1)}, bf16[128,2048]{0,1:T(8,128)(2,1)}, u32[]{:S(2)}, u32[]{:S(2)}) collective-permute-start(bf16[128,2048]{0,1:T(8,128)(2,1)S(1)} %bitcast.105), channel_id=1, source_target_pairs={{0,32},{8,40},{16,48},{24,56},{32,64},{40,72},{48,80},{56,88},{64,... | collective-permute-start | bytes 1572872 | tf_op jit(solution)/shard_map/ppermute | solution.py:15
  96.9 6.0 %copy-start.11 = (bf16[128,16,128]{2,0,1:T(8,128)(2,1)S(1)}, bf16[128,16,128]{2,0,1:T(8,128)(2,1)}, u32[]{:S(2)}) copy-start(bf16[128,16,128]{2,0,1:T(8,128)(2,1)} %copy.32) | copy-start | bytes 1572868
  96.9 6.9 %copy-start.10 = (bf16[128,16,128]{2,0,1:T(8,128)(2,1)S(1)}, bf16[128,16,128]{2,0,1:T(8,128)(2,1)}, u32[]{:S(2)}) copy-start(bf16[128,16,128]{2,0,1:T(8,128)(2,1)} %copy.33) | copy-start | bytes 1572868
  112.3 3.5 copy-start.9
  115.8 1.5 copy-start.5
  117.3 3.3 copy-start.6
  126.9 5.2 %copy-start.8 = (bf16[1,128,2048]{1,2,0:T(8,128)(2,1)S(1)}, bf16[1,128,2048]{1,2,0:T(8,128)(2,1)}, u32[]{:S(2)}) copy-start(bf16[1,128,2048]{1,2,0:T(8,128)(2,1)} %copy.76) | copy-start | bytes 1572868
  132.0 1.5 copy-start.2
  141.0 139.2 %copy-start.7 = (bf16[128,16,128]{0,2,1:T(8,128)(2,1)S(1)}, bf16[128,16,128]{0,2,1:T(8,128)(2,1)}, u32[]{:S(2)}) copy-start(bf16[128,16,128]{0,2,1:T(8,128)(2,1)} %copy.55) | copy-start | bytes 1572868
  143.6 153.2 %collective-permute-start.12 = (f32[128,2048]{0,1:T(8,128)}, f32[128,2048]{0,1:T(8,128)}, u32[]{:S(2)}, u32[]{:S(2)}) collective-permute-start(f32[128,2048]{0,1:T(8,128)} %bitcast.111), channel_id=1, source_target_pairs={{8,0},{16,8},{24,16},{32,24},{40,32},{48,40},{56,48},{64,56},{72,6... | collective-permute-start | bytes 3145736 | tf_op jit(solution)/shard_map/ppermute | solution.py:15
  144.8 153.2 %collective-permute-start.13 = (f32[128,2048]{0,1:T(8,128)}, f32[128,2048]{0,1:T(8,128)}, u32[]{:S(2)}, u32[]{:S(2)}) collective-permute-start(f32[128,2048]{0,1:T(8,128)} %bitcast.110), channel_id=1, source_target_pairs={{16,0},{24,8},{32,16},{40,24},{48,32},{56,40},{64,48},{72,56},{80,... | collective-permute-start | bytes 3145736 | tf_op jit(solution)/shard_map/ppermute | solution.py:15
  146.1 153.2 %collective-permute-start.14 = (f32[128,2048]{0,1:T(8,128)}, f32[128,2048]{0,1:T(8,128)}, u32[]{:S(2)}, u32[]{:S(2)}) collective-permute-start(f32[128,2048]{0,1:T(8,128)} %bitcast.108), channel_id=1, source_target_pairs={{24,0},{32,8},{40,16},{48,24},{56,32},{64,40},{72,48},{80,56},{88,... | collective-permute-start | bytes 3145736 | tf_op jit(solution)/shard_map/ppermute | solution.py:15
  147.5 20.4 %collective-permute-start.20 = (f32[16,128]{1,0:T(8,128)S(1)}, f32[16,128]{1,0:T(8,128)S(1)}, u32[]{:S(2)}, u32[]{:S(2)}) collective-permute-start(f32[16,128]{1,0:T(8,128)S(1)} %get-tuple-element.22), channel_id=1, source_target_pairs={{8,0},{16,8},{24,16},{32,24},{40,32},{48,40},{56,48},{64,56},{72,6... | collective-permute-start | bytes 24584 | tf_op jit(solution)/shard_map/ppermute | solution.py:15
  148.8 130.1 %collective-permute-start.23 = (f32[16,128]{1,0:T(8,128)S(1)}, f32[16,128]{1,0:T(8,128)S(1)}, u32[]{:S(2)}, u32[]{:S(2)}) collective-permute-start(f32[16,128]{1,0:T(8,128)S(1)} %get-tuple-element.23), channel_id=1, source_target_pairs={{32,0},{40,8},{48,16},{56,24},{64,32},{72,40},{80,48},{88,56},{96,... | collective-permute-start | bytes 24584 | tf_op jit(solution)/shard_map/ppermute | solution.py:15
  167.9 116.2 %collective-permute-start.22 = (f32[16,128]{1,0:T(8,128)S(1)}, f32[16,128]{1,0:T(8,128)S(1)}, u32[]{:S(2)}, u32[]{:S(2)}) collective-permute-start(f32[16,128]{1,0:T(8,128)S(1)} %get-tuple-element.24), channel_id=1, source_target_pairs={{24,0},{32,8},{40,16},{48,24},{56,32},{64,40},{72,48},{80,56},{88,... | collective-permute-start | bytes 24584 | tf_op jit(solution)/shard_map/ppermute | solution.py:15
  278.9 205.8 %collective-permute-start.15 = (f32[128,2048]{0,1:T(8,128)}, f32[128,2048]{0,1:T(8,128)}, u32[]{:S(2)}, u32[]{:S(2)}) collective-permute-start(f32[128,2048]{0,1:T(8,128)} %bitcast.109), channel_id=1, source_target_pairs={{32,0},{40,8},{48,16},{56,24},{64,32},{72,40},{80,48},{88,56},{96,... | collective-permute-start | bytes 3145736 | tf_op jit(solution)/shard_map/ppermute | solution.py:15
  284.0 11.4 %collective-permute-start.21 = (f32[16,128]{1,0:T(8,128)S(1)}, f32[16,128]{1,0:T(8,128)S(1)}, u32[]{:S(2)}, u32[]{:S(2)}) collective-permute-start(f32[16,128]{1,0:T(8,128)S(1)} %get-tuple-element.25), channel_id=1, source_target_pairs={{16,0},{24,8},{32,16},{40,24},{48,32},{56,40},{64,48},{72,56},{80,... | collective-permute-start | bytes 24584 | tf_op jit(solution)/shard_map/ppermute | solution.py:15
  290.2 10.5 %copy-start.3 = (bf16[16,128,640]{1,2,0:T(8,128)(2,1)S(1)}, bf16[16,128,640]{1,2,0:T(8,128)(2,1)}, u32[]{:S(2)}) copy-start(bf16[16,128,640]{1,2,0:T(8,128)(2,1)} %copy-done.2) | copy-start | bytes 7864324
  295.5 192.7 %collective-permute-start.17 = (f32[128,2048]{1,0:T(8,128)}, f32[128,2048]{1,0:T(8,128)}, u32[]{:S(2)}, u32[]{:S(2)}) collective-permute-start(f32[128,2048]{1,0:T(8,128)} %copy.58), channel_id=1, source_target_pairs={{16,0},{24,8},{32,16},{40,24},{48,32},{56,40},{64,48},{72,56},{80,... | collective-permute-start | bytes 3145736 | tf_op jit(solution)/shard_map/ppermute | solution.py:15
  296.8 191.4 %collective-permute-start.18 = (f32[128,2048]{1,0:T(8,128)}, f32[128,2048]{1,0:T(8,128)}, u32[]{:S(2)}, u32[]{:S(2)}) collective-permute-start(f32[128,2048]{1,0:T(8,128)} %copy.59), channel_id=1, source_target_pairs={{24,0},{32,8},{40,16},{48,24},{56,32},{64,40},{72,48},{80,56},{88,... | collective-permute-start | bytes 3145736 | tf_op jit(solution)/shard_map/ppermute | solution.py:15
  298.1 190.1 %collective-permute-start.19 = (f32[128,2048]{1,0:T(8,128)}, f32[128,2048]{1,0:T(8,128)}, u32[]{:S(2)}, u32[]{:S(2)}) collective-permute-start(f32[128,2048]{1,0:T(8,128)} %copy.60), channel_id=1, source_target_pairs={{32,0},{40,8},{48,16},{56,24},{64,32},{72,40},{80,48},{88,56},{96,... | collective-permute-start | bytes 3145736 | tf_op jit(solution)/shard_map/ppermute | solution.py:15
  299.4 188.7 %collective-permute-start.16 = (f32[128,2048]{1,0:T(8,128)}, f32[128,2048]{1,0:T(8,128)}, u32[]{:S(2)}, u32[]{:S(2)}) collective-permute-start(f32[128,2048]{1,0:T(8,128)} %copy.56), channel_id=1, source_target_pairs={{8,0},{16,8},{24,16},{32,24},{40,32},{48,40},{56,48},{64,56},{72,6... | collective-permute-start | bytes 3145736 | tf_op jit(solution)/shard_map/ppermute | solution.py:15
  303.4 2.6 copy-start.4
  303.5 3.0 copy-start.14
  487.1 4.5 copy-start.1
where the time goes:
time: 493 us; the launch traced here: 492 us
  blocking collectives  178 us (36%)
  waiting for transfers between devices  137 us (28%)
  starting transfers between devices  80.2 us (16%)
  local copies, waits for them, and re-layouts  63.1 us (13%)
  matrix products  20.4 us (4%)
  other arithmetic  10.9 us (2%)
    psum x1, blocking collectives, shards(): bias_total = lax.psum(bias_local, ('seq', 'dp'))  178 us
    ppermute x24, waiting for transfers between devices, passed_along(): lax.ppermute(value, axis, [(source, source + steps) for source in range(f...  137 us
    ppermute x24, starting transfers between devices, passed_along(): lax.ppermute(value, axis, [(source, source + steps) for source in range(f...  80.2 us
    unnamed x48, local copies, waits for them, and re-layouts  20.6 us
    slice x4, local copies, waits for them, and re-layouts, shards(): grad_key[first_row:first_row + tok_rows]  10.2 us
    slice x5, local copies, waits for them, and re-layouts, shards(): grad_value[first_row:first_row + tok_rows]  9.92 us
  transfers between devices with their start and end apart: 24, of which 5 were waited for; matrix products, arithmetic and copies ran while one was open for 8% of the time, Pallas kernels for 0%

commit v1 on v0

--- a/solution.py
+++ b/solution.py
@@ -7,6 +7,11 @@
 HEAD_DIM = 128
 WINDOW = 512
 FIELDS = 64
+
+
+def by_each_axis(x, leading, second):
+    partial = lax.psum(x, leading)
+    return lax.psum(partial, second)
 
 
 def passed_along(value, axis, steps):
@@ -124,7 +129,7 @@
     query_low = grad_query.reshape(tok_rows, row_width).astype(jnp.bfloat16)
     key_low = key_total.astype(jnp.bfloat16)
     value_low = value_total.astype(jnp.bfloat16)
-    bias_total = lax.psum(bias_local, ("seq", "dp"))
+    bias_total = by_each_axis(bias_local, "dp", "seq")
     return (
         query_low.reshape(1, tok_rows, row_width),
         key_low.reshape(1, tok_rows, row_width),

time: 493 us -> 554 us (1.12)
  the two profiles are of different devices: /device:TPU:1 before, /device:TPU:134 now
where the time goes in v1:
time: 554 us; the launch traced here: 552 us
  blocking collectives  221 us (40%)
  starting transfers between devices  133 us (24%)
  waiting for transfers between devices  102 us (18%)
  local copies, waits for them, and re-layouts  62.8 us (11%)
  matrix products  20.4 us (4%)
  other arithmetic  10.9 us (2%)
    psum x1, blocking collectives, by_each_axis(): return lax.psum(partial, second)  210 us
    ppermute x24, starting transfers between devices, passed_along(): lax.ppermute(value, axis, [(source, source + steps) for source in range(f...  133 us
    ppermute x24, waiting for transfers between devices, passed_along(): lax.ppermute(value, axis, [(source, source + steps) for source in range(f...  102 us
    unnamed x48, local copies, waits for them, and re-layouts  20.5 us
  transfers between devices with their start and end apart: 24, of which 5 were waited for; matrix products, arithmetic and copies ran while one was open for 8% of the time, Pallas kernels for 0%

profile of v1, /device:TPU:134, one launch (start us, length us, event | category | flops | bytes accessed | tf_op | source)
XLA Modules:
  0.0 552.4 jit_solution(16666128271713115883)
XLA Ops:
  2.2 3.6 collective-permute-start.7
  5.8 4.8 collective-permute-start.6
  12.0 2.9 collective-permute-start.11
  14.8 5.1 collective-permute-start.10
  20.0 3.7 collective-permute-start.9
  24.4 3.7 collective-permute-start.5
  28.1 5.0 collective-permute-start.4
  39.2 2.9 collective-permute-start.8
  42.2 21.8 %collective-permute-start.3 = (bf16[128,2048]{0,1:T(8,128)(2,1)S(1)}, bf16[128,2048]{0,1:T(8,128)(2,1)}, u32[]{:S(2)}, u32[]{:S(2)}) collective-permute-start(bf16[128,2048]{0,1:T(8,128)(2,1)S(1)} %bitcast.102), channel_id=1, source_target_pairs={{0,8},{8,16},{16,24},{24,32},{32,40},{40,48},{48,56},{56,64},{64,7... | collective-permute-start | bytes 1572872 | tf_op jit(solution)/shard_map/ppermute | solution.py:20
  64.0 9.1 %collective-permute-start.2 = (bf16[128,2048]{0,1:T(8,128)(2,1)S(1)}, bf16[128,2048]{0,1:T(8,128)(2,1)}, u32[]{:S(2)}, u32[]{:S(2)}) collective-permute-start(bf16[128,2048]{0,1:T(8,128)(2,1)S(1)} %bitcast.103), channel_id=1, source_target_pairs={{0,16},{8,24},{16,32},{24,40},{32,48},{40,56},{48,64},{56,72},{64,... | collective-permute-start | bytes 1572872 | tf_op jit(solution)/shard_map/ppermute | solution.py:20
  73.1 5.9 %collective-permute-start.1 = (bf16[128,2048]{0,1:T(8,128)(2,1)S(1)}, bf16[128,2048]{0,1:T(8,128)(2,1)}, u32[]{:S(2)}, u32[]{:S(2)}) collective-permute-start(bf16[128,2048]{0,1:T(8,128)(2,1)S(1)} %bitcast.104), channel_id=1, source_target_pairs={{0,24},{8,32},{16,40},{24,48},{32,56},{40,64},{48,72},{56,80},{64,... | collective-permute-start | bytes 1572872 | tf_op jit(solution)/shard_map/ppermute | solution.py:20
  79.0 2.2 collective-permute-start
  83.4 2.0 copy.38
  86.4 11.5 %collective-permute-done.3 = bf16[128,2048]{0,1:T(8,128)(2,1)} collective-permute-done((bf16[128,2048]{0,1:T(8,128)(2,1)S(1)}, bf16[128,2048]{0,1:T(8,128)(2,1)}, u32[]{:S(2)}, u32[]{:S(2)}) %collective-permute-start.3) | collective-permute-done | bytes 524320 | tf_op jit(solution)/shard_map/ppermute | solution.py:20
  97.9 2.0 copy.32
  100.0 2.0 copy.31
  102.0 2.0 copy.30
  107.4 2.0 constant_dynamic-update-slice_fusion.3
  109.4 1.9 constant_dynamic-update-slice_fusion.2
  113.1 7.6 %fusion.34 = (f32[16,128]{1,0:T(8,128)S(1)}, f32[16,128,640]{1,2,0:T(8,128)}) fusion(f32[16,640]{1,0:T(8,128)S(1)} %convert_element_type.46, pred[128,640]{0,1:T(8,128)(4,1)S(1)} %and_and_fusion, bf16[640,16,128]{2,0,1:T(8,128)(2,1)} %constant_dynamic-update-slice_fusion, bf16[128,16,128]{0,2,1:T(8,128)(2,1)} %bitcast.94), kind=kOutput, calls=%fused_computation.67 | convolution fusion | flops 681575040 | bytes 8519680 | tf_op jit(solution)/shard_map/sub | solution.py:87
  125.8 3.3 fusion.8
  129.1 1.9 convolution_bitcast_fusion.1
  131.0 2.6 copy.69
  135.3 5.2 fusion.35
  142.0 2.3 fusion.32
  144.3 2.5 copy.52
  146.8 2.5 copy.51
  149.4 2.6 copy.50
  151.9 30.0 %collective-permute-start.12 = (f32[128,2048]{0,1:T(8,128)}, f32[128,2048]{0,1:T(8,128)}, u32[]{:S(2)}, u32[]{:S(2)}) collective-permute-start(f32[128,2048]{0,1:T(8,128)} %bitcast.111), channel_id=1, source_target_pairs={{8,0},{16,8},{24,16},{32,24},{40,32},{48,40},{56,48},{64,56},{72,6... | collective-permute-start | bytes 3145736 | tf_op jit(solution)/shard_map/ppermute | solution.py:20
  182.0 1.9 collective-permute-start.13
  183.9 1.9 collective-permute-start.14
  185.8 2.8 collective-permute-start.20
  188.6 4.0 collective-permute-start.23
  192.6 2.6 copy.53
  195.2 80.6 %collective-permute-done.20 = f32[16,128]{1,0:T(8,128)S(1)} collective-permute-done((f32[16,128]{1,0:T(8,128)S(1)}, f32[16,128]{1,0:T(8,128)S(1)}, u32[]{:S(2)}, u32[]{:S(2)}) %collective-permute-start.20) | collective-permute-done | bytes 8224 | tf_op jit(solution)/shard_map/ppermute | solution.py:20
  277.7 4.9 collective-permute-done.23
  285.6 3.1 collective-permute-done.22
  288.8 3.5 collective-permute-start.21
  292.3 2.0 fusion.31
  296.9 2.7 copy.59
  299.6 2.6 copy.58
  304.1 8.0 %collective-permute-start.17 = (f32[128,2048]{1,0:T(8,128)}, f32[128,2048]{1,0:T(8,128)}, u32[]{:S(2)}, u32[]{:S(2)}) collective-permute-start(f32[128,2048]{1,0:T(8,128)} %copy.58), channel_id=1, source_target_pairs={{16,0},{24,8},{32,16},{40,24},{48,32},{56,40},{64,48},{72,56},{80,... | collective-permute-start | bytes 3145736 | tf_op jit(solution)/shard_map/ppermute | solution.py:20
  315.9 2.8 collective-permute-start.16
  318.8 2.8 fusion.11
  324.7 11.1 %psum.14 = f32[16,64]{1,0:T(8,128)S(1)} all-reduce(f32[16,64]{1,0:T(8,128)S(1)} %fusion.22), channel_id=1, replica_groups=mesh['seq'=64,'dp'=8] {'dp'}, use_global_device_ids=true, to_apply=%region_3.4 | all-reduce | flops 1024 | bytes 8192 | tf_op jit(solution)/shard_map/psum | solution.py:13
  335.8 209.7 %psum.15 = f32[16,64]{1,0:T(8,128)} all-reduce(f32[16,64]{1,0:T(8,128)S(1)} %psum.14), channel_id=1, replica_groups=mesh['seq'=64,'dp'=8] {'seq'}, use_global_device_ids=true, to_apply=%region_4.5 | all-reduce | flops 1024 | bytes 8192 | tf_op jit(solution)/shard_map/psum | solution.py:14
  545.5 2.4 fusion.18
  549.0 3.4 fusion.19
  (98 shorter events, 42.7 us)
Async XLA Ops:
  0.6 0.7 copy-start
  0.6 36.2 %copy-start.12 = (bf16[1,128,2048]{2,1,0:T(8,128)(2,1)S(1)}, bf16[1,128,2048]{2,1,0:T(8,128)(2,1)}, u32[]{:S(2)}) copy-start(bf16[1,128,2048]{2,1,0:T(8,128)(2,1)} %param.7) | copy-start | bytes 1572868
  2.2 35.7 %copy-start.13 = (bf16[1,128,2048]{2,1,0:T(8,128)(2,1)S(1)}, bf16[1,128,2048]{2,1,0:T(8,128)(2,1)}, u32[]{:S(2)}) copy-start(bf16[1,128,2048]{2,1,0:T(8,128)(2,1)} %param.10) | copy-start | bytes 1572868
  2.2 22.2 %collective-permute-start.7 = (bf16[16,128]{1,0:T(8,128)(2,1)S(1)}, bf16[16,128]{1,0:T(8,128)(2,1)S(1)}, u32[]{:S(2)}, u32[]{:S(2)}) collective-permute-start(bf16[16,128]{1,0:T(8,128)(2,1)S(1)} %fusion.14), channel_id=1, source_target_pairs={{0,8},{8,16},{16,24},{24,32},{32,40},{40,48},{48,56},{56,64},{64,7... | collective-permute-start | bytes 12296 | tf_op jit(solution)/shard_map/ppermute | solution.py:20
  5.8 22.3 %collective-permute-start.6 = (bf16[16,128]{1,0:T(8,128)(2,1)S(1)}, bf16[16,128]{1,0:T(8,128)(2,1)S(1)}, u32[]{:S(2)}, u32[]{:S(2)}) collective-permute-start(bf16[16,128]{1,0:T(8,128)(2,1)S(1)} %fusion.14), channel_id=1, source_target_pairs={{0,16},{8,24},{16,32},{24,40},{32,48},{40,56},{48,64},{56,72},{64,... | collective-permute-start | bytes 12296 | tf_op jit(solution)/shard_map/ppermute | solution.py:20
  12.0 52.0 %collective-permute-start.11 = (bf16[128,2048]{0,1:T(8,128)(2,1)S(1)}, bf16[128,2048]{0,1:T(8,128)(2,1)S(1)}, u32[]{:S(2)}, u32[]{:S(2)}) collective-permute-start(bf16[128,2048]{0,1:T(8,128)(2,1)S(1)} %bitcast.96), channel_id=1, source_target_pairs={{0,8},{8,16},{16,24},{24,32},{32,40},{40,48},{48,56},{56,64},{64,7... | collective-permute-start | bytes 1572872 | tf_op jit(solution)/shard_map/ppermute | solution.py:20
  14.8 58.2 %collective-permute-start.10 = (bf16[128,2048]{0,1:T(8,128)(2,1)S(1)}, bf16[128,2048]{0,1:T(8,128)(2,1)S(1)}, u32[]{:S(2)}, u32[]{:S(2)}) collective-permute-start(bf16[128,2048]{0,1:T(8,128)(2,1)S(1)} %bitcast.97), channel_id=1, source_target_pairs={{0,16},{8,24},{16,32},{24,40},{32,48},{40,56},{48,64},{56,72},{64,... | collective-permute-start | bytes 1572872 | tf_op jit(solution)/shard_map/ppermute | solution.py:20
  20.0 59.0 %collective-permute-start.9 = (bf16[128,2048]{0,1:T(8,128)(2,1)S(1)}, bf16[128,2048]{0,1:T(8,128)(2,1)}, u32[]{:S(2)}, u32[]{:S(2)}) collective-permute-start(bf16[128,2048]{0,1:T(8,128)(2,1)S(1)} %bitcast.98), channel_id=1, source_target_pairs={{0,24},{8,32},{16,40},{24,48},{32,56},{40,64},{48,72},{56,80},{64,... | collective-permute-start | bytes 1572872 | tf_op jit(solution)/shard_map/ppermute | solution.py:20
  24.4 14.8 %collective-permute-start.5 = (bf16[16,128]{1,0:T(8,128)(2,1)S(1)}, bf16[16,128]{1,0:T(8,128)(2,1)S(1)}, u32[]{:S(2)}, u32[]{:S(2)}) collective-permute-start(bf16[16,128]{1,0:T(8,128)(2,1)S(1)} %fusion.14), channel_id=1, source_target_pairs={{0,24},{8,32},{16,40},{24,48},{32,56},{40,64},{48,72},{56,80},{64,... | collective-permute-start | bytes 12296 | tf_op jit(solution)/shard_map/ppermute | solution.py:20
  28.1 14.0 %collective-permute-start.4 = (bf16[16,128]{1,0:T(8,128)(2,1)S(1)}, bf16[16,128]{1,0:T(8,128)(2,1)S(1)}, u32[]{:S(2)}, u32[]{:S(2)}) collective-permute-start(bf16[16,128]{1,0:T(8,128)(2,1)S(1)} %fusion.14), channel_id=1, source_target_pairs={{0,32},{8,40},{16,48},{24,56},{32,64},{40,72},{48,80},{56,88},{64,... | collective-permute-start | bytes 12296 | tf_op jit(solution)/shard_map/ppermute | solution.py:20
  39.2 46.2 %collective-permute-start.8 = (bf16[128,2048]{0,1:T(8,128)(2,1)S(1)}, bf16[128,2048]{0,1:T(8,128)(2,1)S(1)}, u32[]{:S(2)}, u32[]{:S(2)}) collective-permute-start(bf16[128,2048]{0,1:T(8,128)(2,1)S(1)} %bitcast.100), channel_id=1, source_target_pairs={{0,32},{8,40},{16,48},{24,56},{32,64},{40,72},{48,80},{56,88},{64,... | collective-permute-start | bytes 1572872 | tf_op jit(solution)/shard_map/ppermute | solution.py:20
  42.2 55.8 %collective-permute-start.3 = (bf16[128,2048]{0,1:T(8,128)(2,1)S(1)}, bf16[128,2048]{0,1:T(8,128)(2,1)}, u32[]{:S(2)}, u32[]{:S(2)}) collective-permute-start(bf16[128,2048]{0,1:T(8,128)(2,1)S(1)} %bitcast.102), channel_id=1, source_target_pairs={{0,8},{8,16},{16,24},{24,32},{32,40},{40,48},{48,56},{56,64},{64,7... | collective-permute-start | bytes 1572872 | tf_op jit(solution)/shard_map/ppermute | solution.py:20
  64.0 36.0 %collective-permute-start.2 = (bf16[128,2048]{0,1:T(8,128)(2,1)S(1)}, bf16[128,2048]{0,1:T(8,128)(2,1)}, u32[]{:S(2)}, u32[]{:S(2)}) collective-permute-start(bf16[128,2048]{0,1:T(8,128)(2,1)S(1)} %bitcast.103), channel_id=1, source_target_pairs={{0,16},{8,24},{16,32},{24,40},{32,48},{40,56},{48,64},{56,72},{64,... | collective-permute-start | bytes 1572872 | tf_op jit(solution)/shard_map/ppermute | solution.py:20
  73.1 29.0 %collective-permute-start.1 = (bf16[128,2048]{0,1:T(8,128)(2,1)S(1)}, bf16[128,2048]{0,1:T(8,128)(2,1)}, u32[]{:S(2)}, u32[]{:S(2)}) collective-permute-start(bf16[128,2048]{0,1:T(8,128)(2,1)S(1)} %bitcast.104), channel_id=1, source_target_pairs={{0,24},{8,32},{16,40},{24,48},{32,56},{40,64},{48,72},{56,80},{64,... | collective-permute-start | bytes 1572872 | tf_op jit(solution)/shard_map/ppermute | solution.py:20
  79.0 25.1 %collective-permute-start = (bf16[128,2048]{0,1:T(8,128)(2,1)S(1)}, bf16[128,2048]{0,1:T(8,128)(2,1)}, u32[]{:S(2)}, u32[]{:S(2)}) collective-permute-start(bf16[128,2048]{0,1:T(8,128)(2,1)S(1)} %bitcast.105), channel_id=1, source_target_pairs={{0,32},{8,40},{16,48},{24,56},{32,64},{40,72},{48,80},{56,88},{64,... | collective-permute-start | bytes 1572872 | tf_op jit(solution)/shard_map/ppermute | solution.py:20
  105.4 5.9 %copy-start.11 = (bf16[128,16,128]{2,0,1:T(8,128)(2,1)S(1)}, bf16[128,16,128]{2,0,1:T(8,128)(2,1)}, u32[]{:S(2)}) copy-start(bf16[128,16,128]{2,0,1:T(8,128)(2,1)} %copy.32) | copy-start | bytes 1572868
  105.4 6.8 %copy-start.10 = (bf16[128,16,128]{2,0,1:T(8,128)(2,1)S(1)}, bf16[128,16,128]{2,0,1:T(8,128)(2,1)}, u32[]{:S(2)}) copy-start(bf16[128,16,128]{2,0,1:T(8,128)(2,1)} %copy.33) | copy-start | bytes 1572868
  120.7 3.5 copy-start.9
  124.3 1.5 copy-start.5
  125.8 3.3 copy-start.6
  135.3 5.2 copy-start.8
  140.5 1.5 copy-start.2
  149.4 135.2 %copy-start.7 = (bf16[128,16,128]{0,2,1:T(8,128)(2,1)S(1)}, bf16[128,16,128]{0,2,1:T(8,128)(2,1)}, u32[]{:S(2)}) copy-start(bf16[128,16,128]{0,2,1:T(8,128)(2,1)} %copy.55) | copy-start | bytes 1572868
  151.9 160.1 %collective-permute-start.12 = (f32[128,2048]{0,1:T(8,128)}, f32[128,2048]{0,1:T(8,128)}, u32[]{:S(2)}, u32[]{:S(2)}) collective-permute-start(f32[128,2048]{0,1:T(8,128)} %bitcast.111), channel_id=1, source_target_pairs={{8,0},{16,8},{24,16},{32,24},{40,32},{48,40},{56,48},{64,56},{72,6... | collective-permute-start | bytes 3145736 | tf_op jit(solution)/shard_map/ppermute | solution.py:20
  182.0 132.0 %collective-permute-start.13 = (f32[128,2048]{0,1:T(8,128)}, f32[128,2048]{0,1:T(8,128)}, u32[]{:S(2)}, u32[]{:S(2)}) collective-permute-start(f32[128,2048]{0,1:T(8,128)} %bitcast.110), channel_id=1, source_target_pairs={{16,0},{24,8},{32,16},{40,24},{48,32},{56,40},{64,48},{72,56},{80,... | collective-permute-start | bytes 3145736 | tf_op jit(solution)/shard_map/ppermute | solution.py:20
  183.9 132.0 %collective-permute-start.14 = (f32[128,2048]{0,1:T(8,128)}, f32[128,2048]{0,1:T(8,128)}, u32[]{:S(2)}, u32[]{:S(2)}) collective-permute-start(f32[128,2048]{0,1:T(8,128)} %bitcast.108), channel_id=1, source_target_pairs={{24,0},{32,8},{40,16},{48,24},{56,32},{64,40},{72,48},{80,56},{88,... | collective-permute-start | bytes 3145736 | tf_op jit(solution)/shard_map/ppermute | solution.py:20
  185.8 90.0 %collective-permute-start.20 = (f32[16,128]{1,0:T(8,128)S(1)}, f32[16,128]{1,0:T(8,128)S(1)}, u32[]{:S(2)}, u32[]{:S(2)}) collective-permute-start(f32[16,128]{1,0:T(8,128)S(1)} %get-tuple-element.22), channel_id=1, source_target_pairs={{8,0},{16,8},{24,16},{32,24},{40,32},{48,40},{56,48},{64,56},{72,6... | collective-permute-start | bytes 24584 | tf_op jit(solution)/shard_map/ppermute | solution.py:20
  188.6 94.0 %collective-permute-start.23 = (f32[16,128]{1,0:T(8,128)S(1)}, f32[16,128]{1,0:T(8,128)S(1)}, u32[]{:S(2)}, u32[]{:S(2)}) collective-permute-start(f32[16,128]{1,0:T(8,128)S(1)} %get-tuple-element.23), channel_id=1, source_target_pairs={{32,0},{40,8},{48,16},{56,24},{64,32},{72,40},{80,48},{88,56},{96,... | collective-permute-start | bytes 24584 | tf_op jit(solution)/shard_map/ppermute | solution.py:20
  275.8 12.9 %collective-permute-start.22 = (f32[16,128]{1,0:T(8,128)S(1)}, f32[16,128]{1,0:T(8,128)S(1)}, u32[]{:S(2)}, u32[]{:S(2)}) collective-permute-start(f32[16,128]{1,0:T(8,128)S(1)} %get-tuple-element.24), channel_id=1, source_target_pairs={{24,0},{32,8},{40,16},{48,24},{56,32},{64,40},{72,48},{80,56},{88,... | collective-permute-start | bytes 24584 | tf_op jit(solution)/shard_map/ppermute | solution.py:20
  282.7 262.8 %collective-permute-start.15 = (f32[128,2048]{0,1:T(8,128)}, f32[128,2048]{0,1:T(8,128)}, u32[]{:S(2)}, u32[]{:S(2)}) collective-permute-start(f32[128,2048]{0,1:T(8,128)} %bitcast.109), channel_id=1, source_target_pairs={{32,0},{40,8},{48,16},{56,24},{64,32},{72,40},{80,48},{88,56},{96,... | collective-permute-start | bytes 3145736 | tf_op jit(solution)/shard_map/ppermute | solution.py:20
  288.8 15.3 %collective-permute-start.21 = (f32[16,128]{1,0:T(8,128)S(1)}, f32[16,128]{1,0:T(8,128)S(1)}, u32[]{:S(2)}, u32[]{:S(2)}) collective-permute-start(f32[16,128]{1,0:T(8,128)S(1)} %get-tuple-element.25), channel_id=1, source_target_pairs={{16,0},{24,8},{32,16},{40,24},{48,32},{56,40},{64,48},{72,56},{80,... | collective-permute-start | bytes 24584 | tf_op jit(solution)/shard_map/ppermute | solution.py:20
  296.9 21.8 %copy-start.3 = (bf16[16,128,640]{1,2,0:T(8,128)(2,1)S(1)}, bf16[16,128,640]{1,2,0:T(8,128)(2,1)}, u32[]{:S(2)}) copy-start(bf16[16,128,640]{1,2,0:T(8,128)(2,1)} %copy-done.2) | copy-start | bytes 7864324
  304.1 244.9 %collective-permute-start.17 = (f32[128,2048]{1,0:T(8,128)}, f32[128,2048]{1,0:T(8,128)}, u32[]{:S(2)}, u32[]{:S(2)}) collective-permute-start(f32[128,2048]{1,0:T(8,128)} %copy.58), channel_id=1, source_target_pairs={{16,0},{24,8},{32,16},{40,24},{48,32},{56,40},{64,48},{72,56},{80,... | collective-permute-start | bytes 3145736 | tf_op jit(solution)/shard_map/ppermute | solution.py:20
  312.1 236.9 %collective-permute-start.18 = (f32[128,2048]{1,0:T(8,128)}, f32[128,2048]{1,0:T(8,128)}, u32[]{:S(2)}, u32[]{:S(2)}) collective-permute-start(f32[128,2048]{1,0:T(8,128)} %copy.59), channel_id=1, source_target_pairs={{24,0},{32,8},{40,16},{48,24},{56,32},{64,40},{72,48},{80,56},{88,... | collective-permute-start | bytes 3145736 | tf_op jit(solution)/shard_map/ppermute | solution.py:20
  314.0 235.0 %collective-permute-start.19 = (f32[128,2048]{1,0:T(8,128)}, f32[128,2048]{1,0:T(8,128)}, u32[]{:S(2)}, u32[]{:S(2)}) collective-permute-start(f32[128,2048]{1,0:T(8,128)} %copy.60), channel_id=1, source_target_pairs={{32,0},{40,8},{48,16},{56,24},{64,32},{72,40},{80,48},{88,56},{96,... | collective-permute-start | bytes 3145736 | tf_op jit(solution)/shard_map/ppermute | solution.py:20
  315.9 233.0 %collective-permute-start.16 = (f32[128,2048]{1,0:T(8,128)}, f32[128,2048]{1,0:T(8,128)}, u32[]{:S(2)}, u32[]{:S(2)}) collective-permute-start(f32[128,2048]{1,0:T(8,128)} %copy.56), channel_id=1, source_target_pairs={{8,0},{16,8},{24,16},{32,24},{40,32},{48,40},{56,48},{64,56},{72,6... | collective-permute-start | bytes 3145736 | tf_op jit(solution)/shard_map/ppermute | solution.py:20
  321.5 2.6 copy-start.4
  321.5 3.0 copy-start.14
  547.9 4.5 copy-start.1
